TPU v7x, 32 devices: a whole 2x2x4 slice. The times are simulated.
32 devices in a mesh: dp: 8 (over z, x), ctx: 4 (over y, core).
Axes of the slice: x: 2, y: 2, z: 4, core: 2. Of those that a mesh axis runs over, the one named last changes fastest.
Arguments:
- tokens: bfloat16 [16, 1024, 768], P('dp', 'ctx'), may hold values from -6 to 6
- segment_ids: int32 [16, 1024], P('dp', 'ctx'), may hold values from 0 to 3, never falling along the last dimension, each value on 1 to 512 neighbouring positions
- cotangent: bfloat16 [16, 1024, 768], P('dp', 'ctx'), may hold values from -6 to 6
- w_in: float32 [768, 3352], P(('dp', 'ctx')), may hold values from -0.21875 to 0.21875
- w_out: float32 [1536, 768], P(('dp', 'ctx')), may hold values from -0.15625 to 0.15625
- mom_in: float32 [768, 3352], P(('dp', 'ctx')), may hold values from -128 to 128
- mom_out: float32 [1536, 768], P(('dp', 'ctx')), may hold values from -640 to 640
- pre_gain: float32 [768], replicated, may hold values from 0.5 to 1.5
- conv_weight: float32 [4, 1792], replicated, may hold values from -3 to 3
- conv_bias: float32 [1792], replicated, may hold values from -6 to 6
- dt_bias: float32 [24], replicated, may hold values from -5 to -3
- a_log: float32 [24], replicated, may hold values from -3.5 to 1.1
- d_skip: float32 [24], replicated, may hold values from 0.5 to 1.5
- norm_gain: float32 [1536], replicated, may hold values from 0.5 to 1.5
Outputs:
- mixed: bfloat16 [16, 1024, 768], P('dp', 'ctx')
- d_tokens: bfloat16 [16, 1024, 768], P('dp', 'ctx')
- grad_w_in: float32 [768, 3352], P(('dp', 'ctx'))
- grad_w_out: float32 [1536, 768], P(('dp', 'ctx'))
- grad_pre_gain: float32 [768], replicated
- grad_conv_weight: float32 [4, 1792], replicated
- grad_conv_bias: float32 [1792], replicated
- grad_dt_bias: float32 [24], replicated
- grad_a_log: float32 [24], replicated
- grad_d_skip: float32 [24], replicated
- grad_norm_gain: float32 [1536], replicated
- new_w_in: float32 [768, 3352], P(('dp', 'ctx'))
- new_w_out: float32 [1536, 768], P(('dp', 'ctx'))
- new_mom_in: float32 [768, 3352], P(('dp', 'ctx'))
- new_mom_out: float32 [1536, 768], P(('dp', 'ctx'))
- new_pre_gain: float32 [768], replicated
- new_conv_weight: float32 [4, 1792], replicated
- new_conv_bias: float32 [1792], replicated
- new_dt_bias: float32 [24], replicated
- new_a_log: float32 [24], replicated
- new_d_skip: float32 [24], replicated
- new_norm_gain: float32 [1536], replicated
Inputs may be any that keep to these rules, and one draw needn't show every extreme that they name: `segment_ids`: segment numbers never fall along a sequence; each document has 1 to 512 tokens and one has exactly 512.
All inputs are finite; a program needn't handle non-finite values.
Results may differ from a plain program's by a relative error of at most 0.01.
Values may be sent and summed in bfloat16 or wider, within the bound.
No kernel may reach another device: no remote copies, remote signals or barrier semaphores. Data moves between devices by JAX's collectives and lax.ppermute only.
A program may use at most 192 MiB of HBM per device.

v0:
```python
from functools import partial
import math
import jax
import jax.numpy as jnp
from jax import lax
from jax.sharding import PartitionSpec as P

D = 768
HEADS = 24
HEADDIM = 64
NSTATE = 128
CONVK = 4
MICRO = 2
SEQ_MB = 1
DI = 1536
CONVD = 1792
EPROJ = 3352
norm_eps = 1e-05
coef_a = 3.4445
coef_b = -4.775
coef_c = 2.0315
momentum_rate = 0.95
muon_rate = 0.05
plain_rate = 0.003


def from_behind(block, axis, distance):
    devices = range(lax.axis_size(axis))
    route = [(i - distance, i) for i in devices if i - distance in devices]
    return lax.ppermute(block, axis, route)


def prefix(shard, axis, combine, identity):
    peers, here = (lax.axis_size(axis), lax.axis_index(axis))
    everything = jax.tree.map(
        lambda part, kind: lax.all_gather(part.astype(kind), axis),
        shard,
        (jnp.bfloat16, jnp.bfloat16),
    )
    start = jax.tree.map(
        lambda part, zero: jnp.broadcast_to(jnp.asarray(zero, part.dtype), part.shape),
        shard,
        identity,
    )

    def step(k, before):
        reached = k < here
        new = combine(
            before, jax.tree.map(lambda part, own: part[k].astype(own.dtype), everything, shard)
        )
        return jax.tree.map(lambda a, b: jnp.where(reached, a, b), new, before)

    return lax.fori_loop(0, peers, step, start)


def prefix_2(shard, axis, combine, identity):
    peers, here = (lax.axis_size(axis), lax.axis_index(axis))
    everything = jax.tree.map(
        lambda part, kind: lax.all_gather(part.astype(kind), axis),
        shard,
        jax.tree.map(lambda a: jnp.bfloat16 if a.dtype == jnp.float32 else a.dtype, shard),
    )
    start = jax.tree.map(
        lambda part, zero: jnp.broadcast_to(jnp.asarray(zero, part.dtype), part.shape),
        shard,
        identity,
    )

    def step(k, before):
        at = peers - 1 - k
        reached = at > here
        new = combine(
            before, jax.tree.map(lambda part, own: part[at].astype(own.dtype), everything, shard)
        )
        return jax.tree.map(lambda a, b: jnp.where(reached, a, b), new, before)

    return lax.fori_loop(0, peers, step, start)


def pre_norm(x_float, gain_vec):
    mean_sq = jnp.mean(x_float * x_float, axis=-1, keepdims=True)
    return x_float * lax.rsqrt(mean_sq + norm_eps) * gain_vec


def make_masks(seg_float, rim_seg):
    block_len = seg_float.shape[1]
    causal = jnp.arange(block_len)[:, None] >= jnp.arange(block_len)[None, :]
    same_seg = jnp.where(
        causal[None], seg_float[:, :, None] == seg_float[:, None, :], False
    ).astype(jnp.float32)
    end_same = (seg_float == seg_float[:, -1:]).astype(jnp.float32)
    carry_mask = (seg_float == rim_seg[:, -1:]).astype(jnp.float32)
    seg_ext = jnp.concatenate([rim_seg, seg_float], axis=1)
    tap_masks = tuple(
        (
            (seg_ext[:, tap_idx : tap_idx + block_len] == seg_float).astype(jnp.float32)
            for tap_idx in range(CONVK - 1)
        )
    )
    return (same_seg, end_same, carry_mask, tap_masks)


def block_mid(seg_masks, conv_in, dt_raw, rim_vals, conv_weight, conv_bias, dt_bias, a_log):
    same_seg, end_same, carry_mask, tap_masks = seg_masks
    batch_rows = conv_in.shape[0]
    block_len = conv_in.shape[1]
    extended = jnp.concatenate([rim_vals, conv_in], axis=1)
    conv_sum = conv_bias + conv_weight[CONVK - 1] * conv_in
    for tap_idx in range(CONVK - 1):
        conv_sum = (
            conv_sum
            + conv_weight[tap_idx]
            * extended[:, tap_idx : tap_idx + block_len, :]
            * tap_masks[tap_idx][..., None]
        )
    activated = jax.nn.silu(conv_sum)
    x_heads = activated[..., :DI].reshape(batch_rows, block_len, HEADS, HEADDIM)
    b_state = activated[..., DI : DI + NSTATE]
    c_state = activated[..., DI + NSTATE :]
    dt_step = jax.nn.softplus(dt_raw + dt_bias)
    log_decay = -dt_step * jnp.exp(a_log)
    cum_decay = jnp.cumsum(log_decay, axis=1)
    block_decay = jnp.exp(cum_decay[:, -1, :]) * carry_mask[:, -1:]
    end_weights = jnp.exp(cum_decay[:, -1:, :] - cum_decay) * end_same[..., None] * dt_step
    local_state = jnp.einsum(
        "bqh,bqhp,bqn->bhpn", end_weights, x_heads, b_state, precision=lax.Precision.HIGHEST
    )
    return (block_decay, local_state, x_heads, b_state, c_state, dt_step, cum_decay)


def block_out(
    seg_masks, x_heads, b_state, c_state, dt_step, cum_decay, incoming, gate_in, d_skip, norm_gain
):
    same_seg, end_same, carry_mask, tap_masks = seg_masks
    batch_rows = x_heads.shape[0]
    block_len = x_heads.shape[1]
    scores = jnp.einsum("btn,bsn->bts", c_state, b_state, precision=lax.Precision.HIGHEST)
    cum_heads = jnp.swapaxes(cum_decay, 1, 2)
    decay_gap = cum_heads[:, :, :, None] - cum_heads[:, :, None, :]
    keep_mask = same_seg[:, None]
    decay_mat = jnp.exp(jnp.where(keep_mask > 0, decay_gap, 0.0)) * keep_mask
    weight = decay_mat * scores[:, None] * jnp.swapaxes(dt_step, 1, 2)[:, :, None, :]
    y_inner = jnp.einsum("bhts,bshp->bthp", weight, x_heads, precision=lax.Precision.HIGHEST)
    y_carry = jnp.einsum("btn,bhpn->bthp", c_state, incoming, precision=lax.Precision.HIGHEST)
    y_carry = y_carry * (jnp.exp(cum_decay) * carry_mask[..., None])[..., None]
    y_heads = y_inner + y_carry + d_skip[:, None] * x_heads
    gated = y_heads.reshape(batch_rows, block_len, DI) * jax.nn.silu(gate_in)
    return gated * lax.rsqrt(jnp.mean(gated * gated, axis=-1, keepdims=True) + norm_eps) * norm_gain


def combine_states(before_part, after_part):
    return (
        before_part[0] * after_part[0],
        after_part[0][..., None, None] * before_part[1] + after_part[1],
    )


def orthogonal(matrix_low):
    frobenius = jnp.sqrt(jnp.sum(jnp.square(matrix_low.astype(jnp.float32))))
    current = (matrix_low.astype(jnp.float32) / (frobenius + 1e-07)).astype(jnp.bfloat16)
    for turn_idx in range(5):
        gram_mat = jnp.dot(current, current.T, preferred_element_type=jnp.float32).astype(
            jnp.bfloat16
        )
        poly_mat = coef_b * gram_mat.astype(jnp.float32) + coef_c * jnp.dot(
            gram_mat, gram_mat, preferred_element_type=jnp.float32
        )
        poly_mat = poly_mat.astype(jnp.bfloat16)
        current = (
            coef_a * current.astype(jnp.float32)
            + jnp.dot(poly_mat, current, preferred_element_type=jnp.float32)
        ).astype(jnp.bfloat16)
    return current


def body(
    tokens,
    segment_ids,
    cotangent,
    w_in,
    w_out,
    mom_in,
    mom_out,
    pre_gain,
    conv_weight,
    conv_bias,
    dt_bias,
    a_log,
    d_skip,
    norm_gain,
):
    win_low = w_in.astype(jnp.bfloat16)
    wout_low = w_out.astype(jnp.bfloat16)
    block_len = tokens.shape[1]
    rim_rows = CONVK - 1
    stored = []
    mixed_parts = []
    for micro_idx in range(MICRO):
        micro_rows = slice(micro_idx * SEQ_MB, (micro_idx + 1) * SEQ_MB)
        full_in, full_out = (
            lax.all_gather(win_low, ("dp", "ctx"), axis=0, tiled=True),
            lax.all_gather(wout_low, ("dp", "ctx"), axis=0, tiled=True),
        )
        x_float = tokens[micro_rows].astype(jnp.float32)
        seg_float = segment_ids[micro_rows].astype(jnp.float32)
        normed, back_pre = jax.vjp(pre_norm, x_float, pre_gain)
        normed_low = normed.astype(jnp.bfloat16).reshape(-1, D)
        projected = jnp.dot(normed_low, full_in, preferred_element_type=jnp.float32).astype(
            jnp.bfloat16
        )
        projected = projected.reshape(SEQ_MB, block_len, EPROJ)
        gate_in = projected[..., :DI].astype(jnp.float32)
        conv_in = projected[..., DI : DI + CONVD].astype(jnp.float32)
        dt_raw = projected[..., DI + CONVD :].astype(jnp.float32)
        rim_vals, rim_seg = from_behind(
            (conv_in[:, block_len - rim_rows :, :], seg_float[:, block_len - rim_rows :]), "ctx", 1
        )
        seg_masks = make_masks(seg_float, rim_seg)
        mid_out, back_mid = jax.vjp(
            partial(block_mid, seg_masks),
            conv_in,
            dt_raw,
            rim_vals,
            conv_weight,
            conv_bias,
            dt_bias,
            a_log,
        )
        block_decay = mid_out[0]
        local_state = mid_out[1]
        identity = (jnp.ones_like(block_decay), jnp.zeros_like(local_state))
        incoming = prefix((block_decay, local_state), "ctx", combine_states, identity)[1]
        gated_normed, back_out = jax.vjp(
            partial(block_out, seg_masks),
            mid_out[2],
            mid_out[3],
            mid_out[4],
            mid_out[5],
            mid_out[6],
            incoming,
            gate_in,
            d_skip,
            norm_gain,
        )
        gated_low = gated_normed.astype(jnp.bfloat16).reshape(-1, DI)
        result = (
            jnp.dot(gated_low, full_out, preferred_element_type=jnp.float32).reshape(
                SEQ_MB, block_len, D
            )
            + x_float
        )
        mixed_parts.append(result.astype(jnp.bfloat16))
        stored.append((normed_low, gated_low, back_pre, back_mid, back_out, block_decay, incoming))
    acc_in = jnp.zeros((D, EPROJ), jnp.float32)
    acc_out = jnp.zeros((DI, D), jnp.float32)
    acc_pre = jnp.zeros_like(pre_gain)
    acc_convw = jnp.zeros_like(conv_weight)
    acc_convb = jnp.zeros_like(conv_bias)
    acc_dtb = jnp.zeros_like(dt_bias)
    acc_alog = jnp.zeros_like(a_log)
    acc_skip = jnp.zeros_like(d_skip)
    acc_norm = jnp.zeros_like(norm_gain)
    grad_parts = [None] * MICRO
    for micro_idx in reversed(range(MICRO)):
        micro_rows = slice(micro_idx * SEQ_MB, (micro_idx + 1) * SEQ_MB)
        full_in, full_out = (
            lax.all_gather(win_low, ("dp", "ctx"), axis=0, tiled=True),
            lax.all_gather(wout_low, ("dp", "ctx"), axis=0, tiled=True),
        )
        normed_low, gated_low, back_pre, back_mid, back_out, block_decay, incoming = stored[
            micro_idx
        ]
        cot_low = cotangent[micro_rows]
        cot_flat = cot_low.reshape(-1, D)
        acc_out = acc_out + jnp.einsum(
            "td,te->de", gated_low, cot_flat, preferred_element_type=jnp.float32
        )
        grad_gated = jnp.einsum(
            "te,de->td", cot_flat, full_out, preferred_element_type=jnp.float32
        ).reshape(SEQ_MB, block_len, DI)
        g_xh, g_bstate, g_cstate, g_dt, g_cum, g_incoming, g_gate, g_skip, g_norm = back_out(
            grad_gated
        )
        identity = (jnp.ones_like(block_decay), jnp.zeros_like(g_incoming))
        carried = prefix_2((block_decay, g_incoming), "ctx", combine_states, identity)[1]
        g_decay = jnp.sum(carried * incoming, axis=(2, 3))
        g_conv, g_dtraw, g_rim, g_convw, g_convb, g_dtb, g_alog = back_mid(
            (g_decay, carried, g_xh, g_bstate, g_cstate, g_dt, g_cum)
        )
        from_next = from_behind(g_rim, "ctx", -1)
        g_conv = jnp.concatenate(
            [g_conv[:, : block_len - rim_rows], g_conv[:, block_len - rim_rows :] + from_next],
            axis=1,
        )
        g_proj = (
            jnp.concatenate([g_gate, g_conv, g_dtraw], axis=-1)
            .astype(jnp.bfloat16)
            .reshape(-1, EPROJ)
        )
        acc_in = acc_in + jnp.einsum(
            "td,te->de", normed_low, g_proj, preferred_element_type=jnp.float32
        )
        g_normed = jnp.einsum(
            "te,de->td", g_proj, full_in, preferred_element_type=jnp.float32
        ).reshape(SEQ_MB, block_len, D)
        g_x, g_pre = back_pre(g_normed)
        grad_parts[micro_idx] = (cot_low.astype(jnp.float32) + g_x).astype(jnp.bfloat16)
        acc_pre = acc_pre + g_pre
        acc_convw = acc_convw + g_convw
        acc_convb = acc_convb + g_convb
        acc_dtb = acc_dtb + g_dtb
        acc_alog = acc_alog + g_alog
        acc_skip = acc_skip + g_skip
        acc_norm = acc_norm + g_norm
    sum_in, sum_out = (
        lax.psum_scatter(acc_in, ("dp", "ctx"), scatter_dimension=0, tiled=True),
        lax.psum_scatter(acc_out, ("dp", "ctx"), scatter_dimension=0, tiled=True),
    )
    smalls = lax.psum(
        (acc_pre, acc_convw, acc_convb, acc_dtb, acc_alog, acc_skip, acc_norm), ("dp", "ctx")
    )
    next_mom_in = momentum_rate * mom_in + sum_in
    next_mom_out = momentum_rate * mom_out + sum_out
    gathered_in, gathered_out = (
        lax.all_gather(next_mom_in.astype(jnp.bfloat16), ("dp", "ctx"), axis=0, tiled=True),
        lax.all_gather(next_mom_out.astype(jnp.bfloat16), ("dp", "ctx"), axis=0, tiled=True),
    )
    position = lax.axis_index(("dp", "ctx"))
    rows_in = w_in.shape[0]
    rows_out = w_out.shape[0]
    ortho_in = orthogonal(gathered_in)
    ortho_out_full = orthogonal(gathered_out.T).T
    mine_in = lax.dynamic_slice_in_dim(ortho_in, position * rows_in, rows_in, 0)
    mine_out = lax.dynamic_slice_in_dim(ortho_out_full, position * rows_out, rows_out, 0)
    new_w_in = w_in - muon_rate * 0.2 * math.sqrt(max(D, EPROJ)) * mine_in.astype(jnp.float32)
    new_w_out = w_out - muon_rate * 0.2 * math.sqrt(max(DI, D)) * mine_out.astype(jnp.float32)
    grad_pre, grad_convw, grad_convb, grad_dtb, grad_alog, grad_skip, grad_norm = smalls
    return (
        jnp.concatenate(mixed_parts, axis=0),
        jnp.concatenate(grad_parts, axis=0),
        sum_in,
        sum_out,
        grad_pre,
        grad_convw,
        grad_convb,
        grad_dtb,
        grad_alog,
        grad_skip,
        grad_norm,
        new_w_in,
        new_w_out,
        next_mom_in,
        next_mom_out,
        pre_gain - plain_rate * grad_pre,
        conv_weight - plain_rate * grad_convw,
        conv_bias - plain_rate * grad_convb,
        dt_bias - plain_rate * grad_dtb,
        a_log - plain_rate * grad_alog,
        d_skip - plain_rate * grad_skip,
        norm_gain - plain_rate * grad_norm,
    )


def solution(mesh):
    return jax.shard_map(
        body,
        mesh=mesh,
        in_specs=(
            P("dp", "ctx", None),
            P("dp", "ctx"),
            P("dp", "ctx", None),
            P(("dp", "ctx"), None),
            P(("dp", "ctx"), None),
            P(("dp", "ctx"), None),
            P(("dp", "ctx"), None),
            P(),
            P(),
            P(),
            P(),
            P(),
            P(),
            P(),
        ),
        out_specs=(
            P("dp", "ctx", None),
            P("dp", "ctx", None),
            P(("dp", "ctx"), None),
            P(("dp", "ctx"), None),
            P(),
            P(),
            P(),
            P(),
            P(),
            P(),
            P(),
            P(("dp", "ctx"), None),
            P(("dp", "ctx"), None),
            P(("dp", "ctx"), None),
            P(("dp", "ctx"), None),
            P(),
            P(),
            P(),
            P(),
            P(),
            P(),
            P(),
        ),
        check_vma=False,
    )
```

profile of v0, /device:TPU:0, one launch (start us, length us, event | category | flops | bytes accessed | tf_op | source)
XLA Modules:
  0.0 1066.6 jit_solution(15806059566089103764)
XLA Ops:
  31.2 48.6 %all-gather.13.cloned.1.call-done = bf16[768,3352]{1,0:T(8,128)(2,1)} async-done(((bf16[24,3352]{1,0:T(8,128)(2,1)}), bf16[768,3352]{1,0:T(8,128)(2,1)}) %all-gather.13.cloned.1.call-update) | async-done | bytes 5148688 | tf_op jit(solution)/shard_map/all_gather | solution.py:201
  158.7 17.6 %all_gather.55 = bf16[4,1,24]{2,1,0:T(2,128)(2,1)} all-gather(bf16[1,1,24]{2,1,0:T(2,128)(2,1)} %get-tuple-element.980), channel_id=1, replica_groups=mesh['dp'=8,'ctx'=4] {'ctx'}, dimensions={0}, use_global_device_ids=true | all-gather | bytes 240 | tf_op jit(solution)/shard_map/all_gather | solution.py:36
  196.3 7.3 while.61
  206.2 8.5 fusion.82
  220.5 7.4 while.60
  230.5 8.6 fusion.83
  248.7 105.5 %reduce-scatter.5.cloned.1.call-done = f32[48,768]{1,0:T(8,128)} async-done(((f32[1536,768]{1,0:T(8,128)}), f32[48,768]{1,0:T(8,128)}) %reduce-scatter.5.cloned.1.call-update) | async-done | bytes 147472 | tf_op jit(solution)/shard_map/reduce_scatter | solution.py:317
  356.4 57.2 %all-gather.19.cloned.1.call-done = bf16[1536,768]{1,0:T(8,128)(2,1)} async-done(((bf16[48,768]{1,0:T(8,128)(2,1)}), bf16[1536,768]{1,0:T(8,128)(2,1)}) %all-gather.19.cloned.1.call-update) | async-done | bytes 2359312 | tf_op jit(solution)/shard_map/all_gather | solution.py:326
  422.2 7.0 fusion.24
  433.6 6.8 add_convert_fusion.6
  445.1 6.9 add_convert_fusion.5
  456.4 6.9 add_convert_fusion.4
  467.7 6.9 fusion.171
  485.3 47.0 %all-gather.15.cloned.1.call-done = bf16[1536,768]{1,0:T(8,128)(2,1)} async-done(((bf16[48,768]{1,0:T(8,128)(2,1)}), bf16[1536,768]{1,0:T(8,128)(2,1)}) %all-gather.15.cloned.1.call-update) | async-done | bytes 2359312 | tf_op jit(solution)/shard_map/all_gather | solution.py:202
  561.7 12.9 %fusion.28 = (f32[24,256]{1,0:T(8,128)}, f32[24,256]{1,0:T(8,128)}, f32[24,256]{1,0:T(8,128)}, f32[256,256]{1,0:T(8,128)S(1)}) fusion(f32[24,256]{1,0:T(8,128)S(1)} %copy-done.133, f32[256,256]{1,0:T(8,128)} %fusion.221, f32[256,256]{1,0:T(8,128)} %get-tuple-element.1007, f32[24,256]{1,0:T(8,128)S(1)} %copy-done.138, pred[256,256]{1,0:T(8,128)(4,1)S(1)} %copy-done.108, ...), kind=kOutput, calls=%fused_computation.56 | convolution fusion | flops 1231468544 | bytes 4120576 | tf_op jit(solution)/shard_map/transpose(jvp(bhts,bshp->bthp))/dot_general | solution.py:143
  597.2 12.7 %fusion.26 = (f32[24,256]{1,0:T(8,128)}, f32[24,256]{1,0:T(8,128)}, f32[24,256]{1,0:T(8,128)}, f32[256,256]{1,0:T(8,128)S(1)}) fusion(f32[24,256]{1,0:T(8,128)} %copy.447, f32[256,256]{1,0:T(8,128)} %copy-done.84, f32[256,256]{1,0:T(8,128)} %get-tuple-element.1005, f32[24,256]{1,0:T(8,128)} %bitcast_add_fusion.14, ...), kind=kOutput, calls=%fused_computation.54 | convolution fusion | flops 1231468544 | bytes 4120576 | tf_op jit(solution)/shard_map/transpose(jvp(bhts,bshp->bthp))/dot_general | solution.py:143
  630.0 7.6 while.62
  642.6 7.3 while.63
  667.3 8.4 fusion.81
  730.2 143.8 %reduce-scatter.7.cloned.1.call-done = f32[24,3352]{1,0:T(8,128)} async-done(((f32[768,3352]{1,0:T(8,128)}), f32[24,3352]{1,0:T(8,128)}) %reduce-scatter.7.cloned.1.call-update) | async-done | bytes 321808
  893.0 42.5 %all-reduce.25 = (f32[768]{0:T(1024)S(1)}, f32[4,1792]{1,0:T(4,128)S(1)}, f32[1792]{0:T(1024)S(1)}, f32[24]{0:T(128)S(1)}, f32[24]{0:T(128)S(1)}, /*index=5*/f32[24]{0:T(128)S(1)}, f32[1536]{0:T(1024)S(1)}) all-reduce(f32[768]{0:T(1024)S(1)} %add.483, ...), channel_id=1, replica_groups=mesh['dp'=8,'ctx'=4] {'dp','ctx'}, use_global_device_ids=true, to_apply=%region_42.44 | all-reduce | flops 11336 | bytes 90688 | tf_op jit(solution)/shard_map/psum | solution.py:319
  942.3 8.0 copy.500
  956.7 8.6 convolution_convert_fusion.6
  965.3 12.1 %add_convert_fusion.3 = bf16[768,3352]{0,1:T(8,128)(2,1)} fusion(bf16[768,768]{1,0:T(8,128)(2,1)S(1)} %convolution_convert_fusion.6, f32[]{:T(128)S(6)} %add.491, bf16[768,3352]{0,1:T(8,128)(2,1)} %copy.500), kind=kOutput, calls=%fused_computation.19 | convolution fusion | flops 4888842240 | bytes 11476996 | tf_op jit(solution)/shard_map/dot_general | solution.py:171
  977.4 8.2 convolution_convert_fusion.5
  985.6 10.6 add_convert_fusion.2
  996.1 7.9 convolution_convert_fusion.4
  1004.1 10.7 %add_convert_fusion.1 = bf16[768,3352]{0,1:T(8,128)(2,1)} fusion(bf16[768,3352]{0,1:T(8,128)(2,1)} %add_convert_fusion.2, bf16[768,768]{1,0:T(8,128)(2,1)S(1)} %convolution_convert_fusion.4), kind=kOutput, calls=%fused_computation.17 | convolution fusion | flops 4873396224 | bytes 11476992 | tf_op jit(solution)/shard_map/dot_general | solution.py:171
  1014.8 7.9 convolution_convert_fusion.3
  1022.7 10.6 add_convert_fusion
  1033.2 7.9 convolution_convert_fusion.2
  1041.2 10.9 %fusion.314 = f32[768,3352]{0,1:T(8,128)} fusion(bf16[768,3352]{0,1:T(8,128)(2,1)} %add_convert_fusion, bf16[768,768]{1,0:T(8,128)(2,1)S(1)} %convolution_convert_fusion.2), kind=kOutput, calls=%fused_computation.526 | convolution fusion | flops 4863098880 | bytes 16625664 | tf_op jit(solution)/shard_map/dot_general | solution.py:171
  (658 shorter events, 396.2 us)
Async XLA Ops:
  7.2 72.6 %copy-start.31 = (bf16[2,256,768]{2,1,0:T(8,128)(2,1)S(1)}, bf16[2,256,768]{2,1,0:T(8,128)(2,1)}, u32[]{:S(2)}) copy-start(bf16[2,256,768]{2,1,0:T(8,128)(2,1)} %param.23) | copy-start | bytes 2359300
  7.2 72.6 %copy-start.61 = (f32[768]{0:T(1024)S(1)}, f32[768]{0:T(1024)}, u32[]{:S(2)}) copy-start(f32[768]{0:T(1024)} %param.30) | copy-start | bytes 9220
  7.2 72.5 %all-gather.13.cloned.1.call-start = ((), (), s32[]{:S(2)}) async-start(), calls=%async_computation.2 | async-start | bytes 5474304 | tf_op jit(solution)/shard_map/all_gather | solution.py:201
  9.0 187.2 %all-gather.23.cloned.1.call-start = ((), (), s32[]{:S(2)}) async-start(), calls=%async_computation.8 | async-start | bytes 1966080 | tf_op jit(solution)/shard_map/all_gather | solution.py:36
  9.9 14.5 %collective-permute-start.3 = (f32[1,3]{1,0:T(1,128)S(1)}, f32[1,3]{1,0:T(1,128)S(1)}, u32[]{:S(2)}, u32[]{:S(2)}) collective-permute-start(f32[1,3]{1,0:T(1,128)S(1)} %slice.264), channel_id=1, source_target_pairs={{0,1},{1,2},{2,3},{4,5},{5,6},{6,7},{8,9},{9,10},{10,11},{12,13},{... | collective-permute-start | bytes 44 | tf_op jit(solution)/shard_map/ppermute | solution.py:30
  12.4 12.6 %collective-permute-start.1 = (f32[1,3]{1,0:T(1,128)S(1)}, f32[1,3]{1,0:T(1,128)S(1)}, u32[]{:S(2)}, u32[]{:S(2)}) collective-permute-start(f32[1,3]{1,0:T(1,128)S(1)} %slice.244), channel_id=1, source_target_pairs={{0,1},{1,2},{2,3},{4,5},{5,6},{6,7},{8,9},{9,10},{10,11},{12,13},{... | collective-permute-start | bytes 44 | tf_op jit(solution)/shard_map/ppermute | solution.py:30
  20.8 156.3 %copy-start.98 = (f32[1792]{0:T(1024)}, f32[1792]{0:T(1024)S(1)}, u32[]{:S(2)}) copy-start(f32[1792]{0:T(1024)S(1)} %get-tuple-element.880) | copy-start | bytes 21508
  22.7 61.3 %copy-start.110 = (f32[256]{0:T(256)}, f32[256]{0:T(256)S(1)}, u32[]{:S(2)}) copy-start(f32[256]{0:T(256)S(1)} %fusion.262) | copy-start | bytes 3076
  22.8 61.5 %copy-start.150 = (f32[256]{0:T(256)}, f32[256]{0:T(256)S(1)}, u32[]{:S(2)}) copy-start(f32[256]{0:T(256)S(1)} %fusion.260) | copy-start | bytes 3076
  103.1 21.9 %collective-permute-start.2 = (f32[1,3,1792]{2,0,1:T(1,128)}, f32[1,3,1792]{2,0,1:T(1,128)}, u32[]{:S(2)}, u32[]{:S(2)}) collective-permute-start(f32[1,3,1792]{2,0,1:T(1,128)} %copy.455), channel_id=1, source_target_pairs={{0,1},{1,2},{2,3},{4,5},{5,6},{6,7},{8,9},{9,10},{10,11},{12,13},{... | collective-permute-start | bytes 64520 | tf_op jit(solution)/shard_map/ppermute | solution.py:30
  133.7 72.4 %copy-start.3 = (f32[1,256,1536]{1,2,0:T(8,128)}, f32[1,256,1536]{1,2,0:T(8,128)S(1)}, u32[]{:S(2)}) copy-start(f32[1,256,1536]{1,2,0:T(8,128)S(1)} %copy.457) | copy-start | bytes 4718596
  136.9 83.5 %all-gather.21.cloned.1.call-start = ((), (), s32[]{:S(2)}) async-start(), calls=%async_computation.7 | async-start | bytes 1966080 | tf_op jit(solution)/shard_map/all_gather | solution.py:36
  140.2 36.2 %collective-permute-start = (f32[1,3,1792]{2,0,1:T(1,128)}, f32[1,3,1792]{2,0,1:T(1,128)}, u32[]{:S(2)}, u32[]{:S(2)}) collective-permute-start(f32[1,3,1792]{2,0,1:T(1,128)} %copy.441), channel_id=1, source_target_pairs={{0,1},{1,2},{2,3},{4,5},{5,6},{6,7},{8,9},{9,10},{10,11},{12,13},{... | collective-permute-start | bytes 64520 | tf_op jit(solution)/shard_map/ppermute | solution.py:30
  196.2 158.1 %reduce-scatter.5.cloned.1.call-start = ((), (), s32[]{:S(2)}) async-start(), calls=%async_computation.4 | async-start | bytes 4866048 | tf_op jit(solution)/shard_map/reduce_scatter | solution.py:317
  244.4 293.9 %copy-start.146 = (f32[256]{0:T(256)}, f32[256]{0:T(256)S(1)}, u32[]{:S(2)}) copy-start(f32[256]{0:T(256)S(1)} %fusion.261) | copy-start | bytes 3076
  248.7 105.6 %copy-start.96 = (f32[48,768]{1,0:T(8,128)S(1)}, f32[48,768]{1,0:T(8,128)}, u32[]{:S(2)}) copy-start(f32[48,768]{1,0:T(8,128)} %param.29) | copy-start | bytes 442372
  248.7 164.9 %all-gather.19.cloned.1.call-start = ((), (), s32[]{:S(2)}) async-start(), calls=%async_computation.6 | async-start | bytes 2433024 | tf_op jit(solution)/shard_map/all_gather | solution.py:326
  355.9 176.4 %all-gather.15.cloned.1.call-start = ((), (), s32[]{:S(2)}) async-start(), calls=%async_computation.3 | async-start | bytes 2433024 | tf_op jit(solution)/shard_map/all_gather | solution.py:202
  476.3 153.7 %all-gather.25.cloned.1.call-start = ((), (), s32[]{:S(2)}) async-start(), calls=%async_computation.9 | async-start | bytes 1966080 | tf_op jit(solution)/shard_map/all_gather | solution.py:59
  552.2 90.3 %all-gather.27.cloned.1.call-start = ((), (), s32[]{:S(2)}) async-start(), calls=%async_computation.10 | async-start | bytes 1966080 | tf_op jit(solution)/shard_map/all_gather | solution.py:59
  609.9 264.1 %reduce-scatter.7.cloned.1.call-start = ((), (), s32[]{:S(2)}) async-start(), calls=%async_computation.11 | async-start | bytes 10948608
  702.2 17.5 %collective-permute-start.4 = (f32[1,3,1792]{2,0,1:T(1,128)S(1)}, f32[1,3,1792]{2,0,1:T(1,128)S(1)}, u32[]{:S(2)}, u32[]{:S(2)}) collective-permute-start(f32[1,3,1792]{2,0,1:T(1,128)S(1)} %copy.475), channel_id=1, source_target_pairs={{1,0},{2,1},{3,2},{5,4},{6,5},{7,6},{9,8},{10,9},{11,10},{13,12},{... | collective-permute-start | bytes 64520 | tf_op jit(solution)/shard_map/ppermute | solution.py:30
  714.8 5.9 collective-permute-start.5
  730.1 144.0 %copy-start.76 = (f32[24,3352]{1,0:T(8,128)S(1)}, f32[24,3352]{1,0:T(8,128)}, u32[]{:S(2)}) copy-start(f32[24,3352]{1,0:T(8,128)} %param.28) | copy-start | bytes 965380
  730.1 145.8 %copy-start.60 = (f32[24,3352]{1,0:T(8,128)S(1)}, f32[24,3352]{1,0:T(8,128)}, u32[]{:S(2)}) copy-start(f32[24,3352]{1,0:T(8,128)} %param.26) | copy-start | bytes 965380
  730.1 147.6 %copy-start.124 = (f32[1536]{0:T(1024)S(1)}, f32[1536]{0:T(1024)}, u32[]{:S(2)}) copy-start(f32[1536]{0:T(1024)} %get-tuple-element.941) | copy-start | bytes 18436
  730.1 147.7 %copy-start.115 = (f32[1536]{0:T(1024)S(1)}, f32[1536]{0:T(1024)}, u32[]{:S(2)}) copy-start(f32[1536]{0:T(1024)} %get-tuple-element.939) | copy-start | bytes 18436
  730.1 147.9 %copy-start.112 = (f32[1536]{0:T(1024)S(1)}, f32[1536]{0:T(1024)}, u32[]{:S(2)}) copy-start(f32[1536]{0:T(1024)} %get-tuple-element.864) | copy-start | bytes 18436
  730.1 147.9 %copy-start.113 = (f32[1536]{0:T(1024)S(1)}, f32[1536]{0:T(1024)}, u32[]{:S(2)}) copy-start(f32[1536]{0:T(1024)} %get-tuple-element.989) | copy-start | bytes 18436
  730.1 147.9 %copy-start.8 = (f32[1,256,1536]{2,1,0:T(8,128)S(1)}, f32[1,256,1536]{2,1,0:T(8,128)}, u32[]{:S(2)}) copy-start(f32[1,256,1536]{2,1,0:T(8,128)} %copy-done.6) | copy-start | bytes 4718596
  730.1 147.9 %copy-start.149 = (f32[256]{0:T(256)S(1)}, f32[256]{0:T(256)}, u32[]{:S(2)}) copy-start(f32[256]{0:T(256)} %fusion.263) | copy-start | bytes 3076
  730.1 212.2 %all-gather.17.cloned.1.call-start = ((), (), s32[]{:S(2)}) async-start(), calls=%async_computation.5 | async-start | bytes 5474304 | tf_op jit(solution)/shard_map/all_gather | solution.py:325
  (171 other events, 996.5 us)
Sparse Core Ops, SparseCore 0:
  11.4 68.2 all-gather.12
  137.0 18.0 all-gather.22
  196.3 17.5 all-gather.20
  248.8 105.4 reduce-scatter.4
  357.6 55.9 all-gather.18
  476.5 55.8 all-gather.14
  552.4 18.4 all-gather.24
  610.0 18.4 all-gather.26
  730.2 143.7 reduce-scatter.6
  877.3 64.9 all-gather.16
where the time goes:
time: 1080 us; the launch traced here: 1070 us
  waiting for transfers between devices  404 us (37%)
  matrix products  298 us (28%)
  other arithmetic  146 us (14%)
  local copies, waits for them, and re-layouts  116 us (11%)
  blocking collectives  65.8 us (6%)
  between operations  18.7 us (2%)
  starting transfers between devices  16.7 us (2%)
    unnamed x11, waiting for transfers between devices  144 us
    reduce_scatter x1, waiting for transfers between devices, body(): lax.psum_scatter(acc_out, ('dp', 'ctx'), scatter_dimension=0, tiled=True)  106 us
    dot_general x10, matrix products, orthogonal(): jnp.dot(poly_mat, current, preferred_element_type=jnp.float32)  89.3 us
    dot_general x10, matrix products, orthogonal(): jnp.dot(current, current.T, preferred_element_type=jnp.float32)  62.8 us
    dot_general x6, matrix products, block_out(): jnp.einsum('bhts,bshp->bthp', weight, x_heads, precision=lax.Precision.HI...  57.9 us
    all_gather x1, waiting for transfers between devices, body(): lax.all_gather(next_mom_out.astype(jnp.bfloat16), ('dp', 'ctx'), axis=0,...  57.2 us
    all_gather x1, waiting for transfers between devices, body(): lax.all_gather(win_low, ('dp', 'ctx'), axis=0, tiled=True)  48.6 us
    all_gather x1, waiting for transfers between devices, body(): lax.all_gather(wout_low, ('dp', 'ctx'), axis=0, tiled=True)  47 us
  transfers between devices with their start and end apart: 16, of which 6 were waited for; matrix products, arithmetic and copies ran while one was open for 21% of the time, Pallas kernels for 0%

commit v1 on v0

--- a/solution.py
+++ b/solution.py
@@ -22,6 +22,13 @@
 momentum_rate = 0.95
 muon_rate = 0.05
 plain_rate = 0.003
+
+
+def swapped_in(x, axis, dim):
+    size = lax.axis_size(axis)
+    blocks = jnp.stack([x for _ in range(size)])
+    blocks = lax.all_to_all(blocks, axis, split_axis=0, concat_axis=0)
+    return jnp.concatenate(blocks, axis=dim)
 
 
 def from_behind(block, axis, distance):
@@ -199,7 +206,7 @@
         micro_rows = slice(micro_idx * SEQ_MB, (micro_idx + 1) * SEQ_MB)
         full_in, full_out = (
             lax.all_gather(win_low, ("dp", "ctx"), axis=0, tiled=True),
-            lax.all_gather(wout_low, ("dp", "ctx"), axis=0, tiled=True),
+            swapped_in(wout_low, ("dp", "ctx"), 0),
         )
         x_float = tokens[micro_rows].astype(jnp.float32)
         seg_float = segment_ids[micro_rows].astype(jnp.float32)

time: 1080 us -> 1160 us (1.074)
  waiting for transfers between devices: 404 us -> 479 us
    all_to_all x0 -> x1, waiting for transfers between devices: none -> 77 us  [swapped_in(): blocks = lax.all_to_all(blocks, axis, split_axis=0, concat_axis=0)]
  transfers between devices with their start and end apart: 16 -> 17, of which waited for: 6 -> 6; matrix products, arithmetic and copies ran while one was open for 21% -> 20% of each run, Pallas kernels for 0% -> 0%
where the time goes in v1:
time: 1160 us; the launch traced here: 1140 us
  waiting for transfers between devices  479 us (41%)
  matrix products  300 us (26%)
  other arithmetic  146 us (13%)
  local copies, waits for them, and re-layouts  117 us (10%)
  blocking collectives  62.8 us (5%)
  starting transfers between devices  20.4 us (2%)
  between operations  18.4 us (2%)
    unnamed x11, waiting for transfers between devices  144 us
    reduce_scatter x1, waiting for transfers between devices, body(): lax.psum_scatter(acc_out, ('dp', 'ctx'), scatter_dimension=0, tiled=True)  106 us
    dot_general x10, matrix products, orthogonal(): jnp.dot(poly_mat, current, preferred_element_type=jnp.float32)  89.2 us
    all_to_all x1, waiting for transfers between devices, swapped_in(): blocks = lax.all_to_all(blocks, axis, split_axis=0, concat_axis=0)  77 us
    dot_general x10, matrix products, orthogonal(): jnp.dot(current, current.T, preferred_element_type=jnp.float32)  63 us
    dot_general x6, matrix products, block_out(): jnp.einsum('bhts,bshp->bthp', weight, x_heads, precision=lax.Precision.HI...  57.9 us
    all_gather x1, waiting for transfers between devices, body(): lax.all_gather(next_mom_out.astype(jnp.bfloat16), ('dp', 'ctx'), axis=0,...  57.2 us
    all_gather x1, waiting for transfers between devices, body(): lax.all_gather(win_low, ('dp', 'ctx'), axis=0, tiled=True)  48.4 us
  transfers between devices with their start and end apart: 17, of which 6 were waited for; matrix products, arithmetic and copies ran while one was open for 20% of the time, Pallas kernels for 0%

profile of v1, /device:TPU:0, one launch (start us, length us, event | category | flops | bytes accessed | tf_op | source)
XLA Modules:
  0.0 1144.4 jit_solution(1560762918955842990)
XLA Ops:
  31.4 48.4 %all-gather.13.cloned.1.call-done = bf16[768,3352]{1,0:T(8,128)(2,1)} async-done(((bf16[24,3352]{1,0:T(8,128)(2,1)}), bf16[768,3352]{1,0:T(8,128)(2,1)}) %all-gather.13.cloned.1.call-update) | async-done | bytes 5148688 | tf_op jit(solution)/shard_map/all_gather | solution.py:208
  158.2 18.8 %all_gather.53 = bf16[4,1,24]{2,1,0:T(2,128)(2,1)} all-gather(bf16[1,1,24]{2,1,0:T(2,128)(2,1)} %get-tuple-element.980), channel_id=1, replica_groups=mesh['dp'=8,'ctx'=4] {'ctx'}, dimensions={0}, use_global_device_ids=true | all-gather | bytes 240 | tf_op jit(solution)/shard_map/all_gather | solution.py:43
  196.9 7.3 while.61
  206.8 8.5 fusion.82
  221.1 7.2 while.60
  231.0 8.6 fusion.83
  249.2 105.5 %reduce-scatter.5.cloned.1.call-done = f32[48,768]{1,0:T(8,128)} async-done(((f32[1536,768]{1,0:T(8,128)}), f32[48,768]{1,0:T(8,128)}) %reduce-scatter.5.cloned.1.call-update) | async-done | bytes 147472 | tf_op jit(solution)/shard_map/reduce_scatter | solution.py:324
  356.8 57.2 %all-gather.19.cloned.1.call-done = bf16[1536,768]{1,0:T(8,128)(2,1)} async-done(((bf16[48,768]{1,0:T(8,128)(2,1)}), bf16[1536,768]{1,0:T(8,128)(2,1)}) %all-gather.19.cloned.1.call-update) | async-done | bytes 2359312 | tf_op jit(solution)/shard_map/all_gather | solution.py:333
  422.6 7.0 fusion.24
  445.5 6.9 add_convert_fusion.5
  456.9 6.9 add_convert_fusion.4
  468.3 6.9 fusion.171
  485.8 47.1 %all-gather.15.cloned.1.call-done = bf16[1536,768]{1,0:T(8,128)(2,1)} async-done(((bf16[48,768]{1,0:T(8,128)(2,1)}), bf16[1536,768]{1,0:T(8,128)(2,1)}) %all-gather.15.cloned.1.call-update) | async-done | bytes 2359312 | tf_op jit(solution)/shard_map/all_gather | solution.py:275
  562.2 12.9 %fusion.28 = (f32[24,256]{1,0:T(8,128)}, f32[24,256]{1,0:T(8,128)}, f32[24,256]{1,0:T(8,128)}, f32[256,256]{1,0:T(8,128)S(1)}) fusion(f32[24,256]{1,0:T(8,128)S(1)} %copy-done.133, f32[256,256]{1,0:T(8,128)} %fusion.221, f32[256,256]{1,0:T(8,128)} %get-tuple-element.1007, f32[24,256]{1,0:T(8,128)S(1)} %copy-done.138, pred[256,256]{1,0:T(8,128)(4,1)S(1)} %copy-done.108, ...), kind=kOutput, calls=%fused_computation.56 | convolution fusion | flops 1231468544 | bytes 4120576 | tf_op jit(solution)/shard_map/transpose(jvp(bhts,bshp->bthp))/dot_general | solution.py:150
  597.6 12.7 %fusion.26 = (f32[24,256]{1,0:T(8,128)}, f32[24,256]{1,0:T(8,128)}, f32[24,256]{1,0:T(8,128)}, f32[256,256]{1,0:T(8,128)S(1)}) fusion(f32[24,256]{1,0:T(8,128)} %copy.447, f32[256,256]{1,0:T(8,128)} %copy-done.84, f32[256,256]{1,0:T(8,128)} %get-tuple-element.1005, f32[24,256]{1,0:T(8,128)} %bitcast_add_fusion.14, ...), kind=kOutput, calls=%fused_computation.54 | convolution fusion | flops 1231468544 | bytes 4120576 | tf_op jit(solution)/shard_map/transpose(jvp(bhts,bshp->bthp))/dot_general | solution.py:150
  630.4 7.5 while.62
  642.7 7.3 while.63
  667.5 8.4 fusion.81
  730.2 143.9 %reduce-scatter.7.cloned.1.call-done = f32[24,3352]{1,0:T(8,128)} async-done(((f32[768,3352]{1,0:T(8,128)}), f32[24,3352]{1,0:T(8,128)}) %reduce-scatter.7.cloned.1.call-update) | async-done | bytes 321808
  883.5 77.0 %all-to-all-done = bf16[32,48,768]{2,1,0:T(8,128)(2,1)} async-done(((bf16[32,48,768]{2,1,0:T(8,128)(2,1)}), bf16[32,48,768]{2,1,0:T(8,128)(2,1)}, u32[]{:S(2)}, u32[]{:S(2)}) %all-to-all-start) | async-done | bytes 2359328 | tf_op jit(solution)/shard_map/all_to_all | solution.py:30
  976.6 38.9 %all-reduce.25 = (f32[768]{0:T(1024)S(1)}, f32[4,1792]{1,0:T(4,128)S(1)}, f32[1792]{0:T(1024)S(1)}, f32[24]{0:T(128)S(1)}, f32[24]{0:T(128)S(1)}, /*index=5*/f32[24]{0:T(128)S(1)}, f32[1536]{0:T(1024)S(1)}) all-reduce(f32[768]{0:T(1024)S(1)} %add.483, ...), channel_id=1, replica_groups=mesh['dp'=8,'ctx'=4] {'dp','ctx'}, use_global_device_ids=true, to_apply=%region_42.44 | all-reduce | flops 11336 | bytes 90688 | tf_op jit(solution)/shard_map/psum | solution.py:326
  1020.6 8.0 copy.500
  1035.0 8.6 convolution_convert_fusion.6
  1043.5 12.2 %add_convert_fusion.3 = bf16[768,3352]{0,1:T(8,128)(2,1)} fusion(bf16[768,768]{1,0:T(8,128)(2,1)S(1)} %convolution_convert_fusion.6, f32[]{:T(128)S(6)} %add.491, bf16[768,3352]{0,1:T(8,128)(2,1)} %copy.500), kind=kOutput, calls=%fused_computation.19 | convolution fusion | flops 4888842240 | bytes 11476996 | tf_op jit(solution)/shard_map/dot_general | solution.py:178
  1055.7 8.3 convolution_convert_fusion.5
  1064.0 10.5 add_convert_fusion.2
  1074.6 7.9 convolution_convert_fusion.4
  1082.5 10.6 add_convert_fusion.1
  1093.1 7.9 convolution_convert_fusion.3
  1101.1 10.5 add_convert_fusion
  1111.6 7.9 convolution_convert_fusion.2
  1119.5 10.7 fusion.314
  (661 shorter events, 406.7 us)
Async XLA Ops:
  7.2 72.6 %copy-start.30 = (bf16[2,256,768]{2,1,0:T(8,128)(2,1)S(1)}, bf16[2,256,768]{2,1,0:T(8,128)(2,1)}, u32[]{:S(2)}) copy-start(bf16[2,256,768]{2,1,0:T(8,128)(2,1)} %param.23) | copy-start | bytes 2359300
  7.2 72.6 %copy-start.61 = (f32[768]{0:T(1024)S(1)}, f32[768]{0:T(1024)}, u32[]{:S(2)}) copy-start(f32[768]{0:T(1024)} %param.30) | copy-start | bytes 9220
  7.2 72.5 %all-gather.13.cloned.1.call-start = ((), (), s32[]{:S(2)}) async-start(), calls=%async_computation.3 | async-start | bytes 5474304 | tf_op jit(solution)/shard_map/all_gather | solution.py:208
  9.0 187.8 %all-gather.23.cloned.1.call-start = ((), (), s32[]{:S(2)}) async-start(), calls=%async_computation.9 | async-start | bytes 1966080 | tf_op jit(solution)/shard_map/all_gather | solution.py:43
  9.9 14.6 %collective-permute-start.3 = (f32[1,3]{1,0:T(1,128)S(1)}, f32[1,3]{1,0:T(1,128)S(1)}, u32[]{:S(2)}, u32[]{:S(2)}) collective-permute-start(f32[1,3]{1,0:T(1,128)S(1)} %slice.264), channel_id=1, source_target_pairs={{0,1},{1,2},{2,3},{4,5},{5,6},{6,7},{8,9},{9,10},{10,11},{12,13},{... | collective-permute-start | bytes 44 | tf_op jit(solution)/shard_map/ppermute | solution.py:37
  12.4 12.7 %collective-permute-start.1 = (f32[1,3]{1,0:T(1,128)S(1)}, f32[1,3]{1,0:T(1,128)S(1)}, u32[]{:S(2)}, u32[]{:S(2)}) collective-permute-start(f32[1,3]{1,0:T(1,128)S(1)} %slice.244), channel_id=1, source_target_pairs={{0,1},{1,2},{2,3},{4,5},{5,6},{6,7},{8,9},{9,10},{10,11},{12,13},{... | collective-permute-start | bytes 44 | tf_op jit(solution)/shard_map/ppermute | solution.py:37
  20.9 156.8 %copy-start.98 = (f32[1792]{0:T(1024)}, f32[1792]{0:T(1024)S(1)}, u32[]{:S(2)}) copy-start(f32[1792]{0:T(1024)S(1)} %get-tuple-element.880) | copy-start | bytes 21508
  22.8 61.2 %copy-start.110 = (f32[256]{0:T(256)}, f32[256]{0:T(256)S(1)}, u32[]{:S(2)}) copy-start(f32[256]{0:T(256)S(1)} %fusion.262) | copy-start | bytes 3076
  22.9 61.4 %copy-start.150 = (f32[256]{0:T(256)}, f32[256]{0:T(256)S(1)}, u32[]{:S(2)}) copy-start(f32[256]{0:T(256)S(1)} %fusion.260) | copy-start | bytes 3076
  28.9 55.2 %copy-start.158 = (f32[1,256]{1,0:T(1,128)}, f32[1,256]{1,0:T(1,128)S(1)}, u32[]{:S(2)}) copy-start(f32[1,256]{1,0:T(1,128)S(1)} %get-tuple-element.992) | copy-start | bytes 3076
  28.9 55.2 %copy-start.160 = (f32[1,256]{1,0:T(1,128)}, f32[1,256]{1,0:T(1,128)S(1)}, u32[]{:S(2)}) copy-start(f32[1,256]{1,0:T(1,128)S(1)} %get-tuple-element.993) | copy-start | bytes 3076
  103.1 22.0 %collective-permute-start.2 = (f32[1,3,1792]{2,0,1:T(1,128)}, f32[1,3,1792]{2,0,1:T(1,128)}, u32[]{:S(2)}, u32[]{:S(2)}) collective-permute-start(f32[1,3,1792]{2,0,1:T(1,128)} %copy.455), channel_id=1, source_target_pairs={{0,1},{1,2},{2,3},{4,5},{5,6},{6,7},{8,9},{9,10},{10,11},{12,13},{... | collective-permute-start | bytes 64520 | tf_op jit(solution)/shard_map/ppermute | solution.py:37
  133.7 73.0 %copy-start.3 = (f32[1,256,1536]{1,2,0:T(8,128)}, f32[1,256,1536]{1,2,0:T(8,128)S(1)}, u32[]{:S(2)}) copy-start(f32[1,256,1536]{1,2,0:T(8,128)S(1)} %copy.457) | copy-start | bytes 4718596
  137.0 84.1 %all-gather.21.cloned.1.call-start = ((), (), s32[]{:S(2)}) async-start(), calls=%async_computation.8 | async-start | bytes 1966080 | tf_op jit(solution)/shard_map/all_gather | solution.py:43
  140.2 36.7 %collective-permute-start = (f32[1,3,1792]{2,0,1:T(1,128)}, f32[1,3,1792]{2,0,1:T(1,128)}, u32[]{:S(2)}, u32[]{:S(2)}) collective-permute-start(f32[1,3,1792]{2,0,1:T(1,128)} %copy.441), channel_id=1, source_target_pairs={{0,1},{1,2},{2,3},{4,5},{5,6},{6,7},{8,9},{9,10},{10,11},{12,13},{... | collective-permute-start | bytes 64520 | tf_op jit(solution)/shard_map/ppermute | solution.py:37
  196.8 157.9 %reduce-scatter.5.cloned.1.call-start = ((), (), s32[]{:S(2)}) async-start(), calls=%async_computation.5 | async-start | bytes 4866048 | tf_op jit(solution)/shard_map/reduce_scatter | solution.py:324
  244.8 294.0 %copy-start.146 = (f32[256]{0:T(256)}, f32[256]{0:T(256)S(1)}, u32[]{:S(2)}) copy-start(f32[256]{0:T(256)S(1)} %fusion.261) | copy-start | bytes 3076
  249.1 105.6 %copy-start.96 = (f32[48,768]{1,0:T(8,128)S(1)}, f32[48,768]{1,0:T(8,128)}, u32[]{:S(2)}) copy-start(f32[48,768]{1,0:T(8,128)} %param.29) | copy-start | bytes 442372
  249.1 164.9 %all-gather.19.cloned.1.call-start = ((), (), s32[]{:S(2)}) async-start(), calls=%async_computation.7 | async-start | bytes 2433024 | tf_op jit(solution)/shard_map/all_gather | solution.py:333
  356.4 176.5 %all-gather.15.cloned.1.call-start = ((), (), s32[]{:S(2)}) async-start(), calls=%async_computation.4 | async-start | bytes 2433024 | tf_op jit(solution)/shard_map/all_gather | solution.py:275
  476.9 153.5 %all-gather.25.cloned.1.call-start = ((), (), s32[]{:S(2)}) async-start(), calls=%async_computation.10 | async-start | bytes 1966080 | tf_op jit(solution)/shard_map/all_gather | solution.py:66
  552.7 90.0 %all-gather.27.cloned.1.call-start = ((), (), s32[]{:S(2)}) async-start(), calls=%async_computation.11 | async-start | bytes 1966080 | tf_op jit(solution)/shard_map/all_gather | solution.py:66
  610.3 263.7 %reduce-scatter.7.cloned.1.call-start = ((), (), s32[]{:S(2)}) async-start(), calls=%async_computation.12 | async-start | bytes 10948608
  702.3 17.5 %collective-permute-start.4 = (f32[1,3,1792]{2,0,1:T(1,128)S(1)}, f32[1,3,1792]{2,0,1:T(1,128)S(1)}, u32[]{:S(2)}, u32[]{:S(2)}) collective-permute-start(f32[1,3,1792]{2,0,1:T(1,128)S(1)} %copy.475), channel_id=1, source_target_pairs={{1,0},{2,1},{3,2},{5,4},{6,5},{7,6},{9,8},{10,9},{11,10},{13,12},{... | collective-permute-start | bytes 64520 | tf_op jit(solution)/shard_map/ppermute | solution.py:37
  714.9 5.9 collective-permute-start.5
  730.1 144.0 %copy-start.76 = (f32[24,3352]{1,0:T(8,128)S(1)}, f32[24,3352]{1,0:T(8,128)}, u32[]{:S(2)}) copy-start(f32[24,3352]{1,0:T(8,128)} %param.28) | copy-start | bytes 965380
  730.1 145.8 %copy-start.60 = (bf16[48,768]{1,0:T(8,128)(2,1)S(1)}, bf16[48,768]{1,0:T(8,128)(2,1)}, u32[]{:S(2)}) copy-start(bf16[48,768]{1,0:T(8,128)(2,1)} %get-tuple-element.978) | copy-start | bytes 221188
  730.1 290.5 %all-gather.17.cloned.1.call-start = ((), (), s32[]{:S(2)}) async-start(), calls=%async_computation.6 | async-start | bytes 5474304 | tf_op jit(solution)/shard_map/all_gather | solution.py:332
  877.5 83.0 %all-to-all-start = ((bf16[32,48,768]{2,1,0:T(8,128)(2,1)}), bf16[32,48,768]{2,1,0:T(8,128)(2,1)}, u32[]{:S(2)}, u32[]{:S(2)}) async-start(bf16[32,48,768]{2,1,0:T(8,128)(2,1)} %stack.2), calls=%async_computation | async-start | bytes 4718592 | tf_op jit(solution)/shard_map/all_to_all | solution.py:30
  881.3 79.2 %copy-start.8 = (f32[1,256,1536]{2,1,0:T(8,128)S(1)}, f32[1,256,1536]{2,1,0:T(8,128)}, u32[]{:S(2)}) copy-start(f32[1,256,1536]{2,1,0:T(8,128)} %copy-done.6) | copy-start | bytes 4718596
  881.3 79.2 %copy-start.149 = (f32[256]{0:T(256)S(1)}, f32[256]{0:T(256)}, u32[]{:S(2)}) copy-start(f32[256]{0:T(256)} %fusion.263) | copy-start | bytes 3076
  972.0 43.6 %copy-start.29 = (bf16[2,256,768]{2,1,0:T(8,128)(2,1)S(1)}, bf16[2,256,768]{2,1,0:T(8,128)(2,1)}, u32[]{:S(2)}) copy-start(bf16[2,256,768]{2,1,0:T(8,128)(2,1)} %param.25) | copy-start | bytes 2359300
  (172 other events, 857.4 us)
Sparse Core Ops, SparseCore 0:
  11.4 68.2 all-gather.12
  137.1 18.0 all-gather.22
  196.9 17.5 all-gather.20
  249.2 105.4 reduce-scatter.4
  358.0 55.9 all-gather.18
  477.0 55.8 all-gather.14
  552.8 18.4 all-gather.24
  610.5 18.4 all-gather.26
  730.2 143.7 reduce-scatter.6
  877.3 83.9 all-gather.16
